TPU v7x, 128 devices: a whole 4x4x4 slice. The times are simulated.
128 devices in a mesh: group: 16 (over y, z), fold: 8 (over x, core).
Axes of the slice: x: 4, y: 4, z: 4, core: 2. Of those that a mesh axis runs over, the one named last changes fastest.
Arguments:
- right_side: float32 [16, 262144], P(None, ('group', 'fold')), may hold values from -6 to 6
- initial: float32 [16, 262144], P(None, ('group', 'fold')), may hold values from -6 to 6
- counts: int32 [16, 8], P('group'), may hold values from 1 to 2048, 8192 in all within a row
- columns: int32 [1024, 5], P('group'), may hold values from 0 to 69, as said below
- blocks: float32 [1024, 5, 128, 128], P('group')
Outputs:
- smoothed: float32 [16, 262144], P(None, ('group', 'fold'))
Inputs may be any that keep to these rules, and one draw needn't show every extreme that they name: Every row of counts sums to 8192, and its largest entry is 2048. `columns`: index j of row block g * 64 + i names block g * 64 + j - 3; the 5 indices of a row block are distinct and lie within 3 of i + 3.
All inputs are finite; a program needn't handle non-finite values.
Results may differ from a plain program's by a relative error of at most 0.0001.
Values sent between devices are 32-bit elements; how exact they have to be, the bound alone decides.
A program may use at most 192 MiB of HBM per device.

v0:
```python
import jax
import jax.numpy as jnp
from jax import lax
from jax.sharding import PartitionSpec as P

HB = 3
SWEEPS = 3
DEGREE = 4
upper_bound = 4.5
lower_bound = 1.35


def padded_2(shard, sides, width):
    for axis, dim in sides:
        devices, length = (lax.axis_size(axis), shard.shape[dim])
        up = [(i, (i + 1) % devices) for i in range(devices - 1)]
        down = [(j, i) for i, j in up]
        last = lax.slice_in_dim(shard, length - width, length, axis=dim)
        initial = lax.slice_in_dim(shard, 0, width, axis=dim)
        before = lax.ppermute(last, axis, up)
        after = lax.ppermute(initial, axis, down)
        shard = jnp.concatenate([before, shard, after], axis=dim)
    return shard


def on_device(right_side, initial, counts, columns, blocks):
    folds = lax.axis_size("fold")
    vectors, capacity = right_side.shape
    own_blocks, width = (blocks.shape[0], blocks.shape[2])
    live_rows = counts[0]
    starts = jnp.cumsum(live_rows) - live_rows
    stacked = jnp.stack([right_side, initial])
    gathered = lax.all_gather(stacked, "fold", axis=2, tiled=True)
    position = lax.axis_index("fold")
    row_ids = jnp.arange(own_blocks * width, dtype=jnp.int32)
    covered = starts[None, :] <= row_ids[:, None]
    owner_slot = jnp.sum(covered.astype(jnp.int32), axis=1) - 1
    row_start = jnp.max(jnp.where(covered, starts[None, :], 0), axis=1)
    source = owner_slot * capacity + row_ids - row_start
    owned = jnp.take(gathered, source, axis=2)
    target = owned[0]
    iterate = owned[1]

    def operate(vector):
        extended = padded_2(vector, (("group", 1),), HB * width)
        extended = extended.reshape(vectors, own_blocks + 2 * HB, width)
        picked = jnp.take(extended, columns, axis=1)
        result = jnp.einsum("nikc,ikrc->nir", picked, blocks, precision=lax.Precision.HIGHEST)
        return result.reshape(vectors, own_blocks * width)

    theta = (upper_bound + lower_bound) / 2.0
    delta = (upper_bound - lower_bound) / 2.0
    for sweep in range(SWEEPS):
        resid = target - operate(iterate)
        update = resid / theta
        ratio_now = delta / theta
        for step in range(DEGREE):
            iterate = iterate + update
            if step + 1 < DEGREE:
                resid = resid - operate(update)
                ratio_next = 1.0 / (2.0 * theta / delta - ratio_now)
                update = ratio_next * ratio_now * update + 2.0 * ratio_next / delta * resid
                ratio_now = ratio_next
    fold_ids = jnp.arange(folds, dtype=jnp.int32)
    my_start = jnp.sum(jnp.where(fold_ids == position, starts, 0))
    my_count = jnp.sum(jnp.where(fold_ids == position, live_rows, 0))
    padded = jnp.concatenate([iterate, jnp.zeros((vectors, capacity), jnp.float32)], axis=1)
    piece = lax.dynamic_slice_in_dim(padded, my_start, capacity, 1)
    valid = jnp.arange(capacity, dtype=jnp.int32) < my_count
    return jnp.where(valid[None, :], piece, jnp.float32(0.0))


def solution(mesh):
    placed = (
        P(None, ("group", "fold")),
        P(None, ("group", "fold")),
        P("group", None),
        P("group", None),
        P("group", None, None, None),
    )
    return jax.shard_map(
        on_device, mesh=mesh, in_specs=placed, out_specs=P(None, ("group", "fold")), check_vma=False
    )
```

profile of v0, /device:TPU:8, one launch (start us, length us, event | category | flops | bytes accessed | tf_op | source)
XLA Modules:
  0.0 559.2 jit_solution(11467768197865809706)
XLA Ops:
  11.8 24.7 %all-gather.2.cloned.1.call-done = f32[2,16,16384]{2,1,0:T(8,128)} async-done(((f32[2,16,2048]{2,1,0:T(8,128)}), f32[2,16,16384]{2,1,0:T(8,128)}) %all-gather.2.cloned.1.call-update) | async-done | bytes 2097168 | tf_op jit(solution)/shard_map/all_gather | solution.py:33
  36.5 18.6 %copy.304 = f32[2,16,16384]{1,0,2:T(2,128)} copy(f32[2,16,16384]{2,1,0:T(8,128)} %all-gather.2.cloned.1.call-done) | data formatting | bytes 4194304 | tf_op jit(solution)/shard_map/all_gather | solution.py:33
  55.2 62.3 %gather_fusion = f32[8192,2,16]{2,1,0:T(2,128)} fusion(f32[2,16,16384]{1,0,2:T(2,128)} %copy.304, s32[8192]{0:T(1024)S(1)} %broadcast_clamp_fusion), kind=kCustom, calls=%fused_computation.12 | custom fusion | bytes 2129920 | tf_op jit(solution)/shard_map/jit(_take)/gather | solution.py:40
  117.4 9.3 %copy.305 = f32[8192,2,16]{0,2,1:T(8,128)S(1)} copy(f32[8192,2,16]{2,1,0:T(2,128)} %gather_fusion) | data formatting | bytes 2097152 | tf_op jit(solution)/shard_map/jit(_take)/gather | solution.py:40
  126.9 3.5 collective-permute-start
  130.4 4.5 collective-permute-start.1
  136.4 1.9 gather_fusion.1
  138.3 23.1 %fusion.60 = f32[64,2,8,128]{3,2,1,0:T(8,128)S(1)} fusion(f32[64,5,128,128]{3,2,1,0:T(8,128)} %param.11, f32[64,5,16,128]{3,2,1,0:T(8,128)S(1)} %bitcast.334, pred[64,5]{1,0:T(8,128)(4,1)S(1)} %copy.306), kind=kOutput, calls=%fused_computation.73 | convolution fusion | flops 1007288320 | bytes 24117568 | tf_op jit(solution)/shard_map/nikc,ikrc->nir/dot_general | solution.py:48
  162.4 3.2 collective-permute-start.2
  165.6 5.3 collective-permute-start.3
  172.2 1.9 gather_fusion.2
  174.1 23.1 %fusion.63 = f32[64,2,8,128]{3,2,1,0:T(8,128)S(1)} fusion(f32[64,5,128,128]{3,2,1,0:T(8,128)} %param.11, f32[64,5,16,128]{3,2,1,0:T(8,128)S(1)} %bitcast.335, pred[64,5]{1,0:T(8,128)(4,1)S(1)} %copy.306), kind=kOutput, calls=%fused_computation.74 | convolution fusion | flops 1007288320 | bytes 24117568 | tf_op jit(solution)/shard_map/nikc,ikrc->nir/dot_general | solution.py:48
  197.3 3.6 collective-permute-start.4
  200.9 4.6 collective-permute-start.5
  207.1 1.9 gather_fusion.3
  209.0 23.1 %fusion.66 = f32[64,2,8,128]{3,2,1,0:T(8,128)S(1)} fusion(f32[64,5,128,128]{3,2,1,0:T(8,128)} %param.11, f32[64,5,16,128]{3,2,1,0:T(8,128)S(1)} %bitcast.336, pred[64,5]{1,0:T(8,128)(4,1)S(1)} %copy.306), kind=kOutput, calls=%fused_computation.75 | convolution fusion | flops 1007288320 | bytes 24117568 | tf_op jit(solution)/shard_map/nikc,ikrc->nir/dot_general | solution.py:48
  232.4 3.6 collective-permute-start.6
  236.0 5.2 collective-permute-start.7
  242.2 1.9 gather_fusion.4
  244.1 23.2 %fusion.69 = f32[64,2,8,128]{3,2,1,0:T(8,128)S(1)} fusion(f32[64,5,128,128]{3,2,1,0:T(8,128)} %param.11, f32[64,5,16,128]{3,2,1,0:T(8,128)S(1)} %bitcast.337, pred[64,5]{1,0:T(8,128)(4,1)S(1)} %copy.306), kind=kOutput, calls=%fused_computation.76 | convolution fusion | flops 1007288320 | bytes 24117568 | tf_op jit(solution)/shard_map/nikc,ikrc->nir/dot_general | solution.py:48
  267.6 3.6 collective-permute-start.8
  271.3 4.6 collective-permute-start.9
  277.4 1.9 gather_fusion.5
  279.4 23.1 %fusion.72 = f32[64,2,8,128]{3,2,1,0:T(8,128)S(1)} fusion(f32[64,5,128,128]{3,2,1,0:T(8,128)} %param.11, f32[64,5,16,128]{3,2,1,0:T(8,128)S(1)} %bitcast.338, pred[64,5]{1,0:T(8,128)(4,1)S(1)} %copy.306), kind=kOutput, calls=%fused_computation.77 | convolution fusion | flops 1007288320 | bytes 24117568 | tf_op jit(solution)/shard_map/nikc,ikrc->nir/dot_general | solution.py:48
  303.4 3.6 collective-permute-start.10
  307.0 4.8 collective-permute-start.11
  313.2 1.9 gather_fusion.6
  315.1 23.1 %fusion.75 = f32[64,2,8,128]{3,2,1,0:T(8,128)S(1)} fusion(f32[64,5,128,128]{3,2,1,0:T(8,128)} %param.11, f32[64,5,16,128]{3,2,1,0:T(8,128)S(1)} %bitcast.339, pred[64,5]{1,0:T(8,128)(4,1)S(1)} %copy.306), kind=kOutput, calls=%fused_computation.78 | convolution fusion | flops 1007288320 | bytes 24117568 | tf_op jit(solution)/shard_map/nikc,ikrc->nir/dot_general | solution.py:48
  338.3 3.6 collective-permute-start.12
  341.9 4.6 collective-permute-start.13
  348.1 1.9 gather_fusion.7
  350.0 23.1 %fusion.78 = f32[64,2,8,128]{3,2,1,0:T(8,128)S(1)} fusion(f32[64,5,128,128]{3,2,1,0:T(8,128)} %param.11, f32[64,5,16,128]{3,2,1,0:T(8,128)S(1)} %bitcast.340, pred[64,5]{1,0:T(8,128)(4,1)S(1)} %copy.306), kind=kOutput, calls=%fused_computation.79 | convolution fusion | flops 1007288320 | bytes 24117568 | tf_op jit(solution)/shard_map/nikc,ikrc->nir/dot_general | solution.py:48
  373.4 3.6 collective-permute-start.14
  377.0 4.8 collective-permute-start.15
  383.2 1.9 gather_fusion.8
  385.1 23.2 %fusion.81 = f32[64,2,8,128]{3,2,1,0:T(8,128)S(1)} fusion(f32[64,5,128,128]{3,2,1,0:T(8,128)} %param.11, f32[64,5,16,128]{3,2,1,0:T(8,128)S(1)} %bitcast.341, pred[64,5]{1,0:T(8,128)(4,1)S(1)} %copy.306), kind=kOutput, calls=%fused_computation.80 | convolution fusion | flops 1007288320 | bytes 24117568 | tf_op jit(solution)/shard_map/nikc,ikrc->nir/dot_general | solution.py:48
  408.6 3.6 collective-permute-start.16
  412.3 4.6 collective-permute-start.17
  420.4 23.1 %fusion.84 = f32[64,2,8,128]{3,2,1,0:T(8,128)S(1)} fusion(f32[64,5,128,128]{3,2,1,0:T(8,128)} %param.11, f32[64,5,16,128]{3,2,1,0:T(8,128)S(1)} %bitcast.342, pred[64,5]{1,0:T(8,128)(4,1)S(1)} %copy.306), kind=kOutput, calls=%fused_computation.81 | convolution fusion | flops 1007288320 | bytes 24117568 | tf_op jit(solution)/shard_map/nikc,ikrc->nir/dot_general | solution.py:48
  444.4 3.6 collective-permute-start.18
  448.0 5.0 collective-permute-start.19
  456.1 23.1 %fusion.87 = f32[64,2,8,128]{3,2,1,0:T(8,128)S(1)} fusion(f32[64,5,128,128]{3,2,1,0:T(8,128)} %param.11, f32[64,5,16,128]{3,2,1,0:T(8,128)S(1)} %bitcast.343, pred[64,5]{1,0:T(8,128)(4,1)S(1)} %copy.306), kind=kOutput, calls=%fused_computation.82 | convolution fusion | flops 1007288320 | bytes 24117568 | tf_op jit(solution)/shard_map/nikc,ikrc->nir/dot_general | solution.py:48
  479.4 3.6 collective-permute-start.20
  483.0 4.6 collective-permute-start.21
  491.1 23.1 %fusion.90 = f32[64,2,8,128]{3,2,1,0:T(8,128)S(1)} fusion(f32[64,5,128,128]{3,2,1,0:T(8,128)} %param.11, f32[64,5,16,128]{3,2,1,0:T(8,128)S(1)} %bitcast.344, pred[64,5]{1,0:T(8,128)(4,1)S(1)} %copy.306), kind=kOutput, calls=%fused_computation.83 | convolution fusion | flops 1007288320 | bytes 24117568 | tf_op jit(solution)/shard_map/nikc,ikrc->nir/dot_general | solution.py:48
  515.1 3.6 collective-permute-start.22
  518.7 4.8 collective-permute-start.23
  527.9 23.2 %fusion.93 = f32[64,2,8,128]{3,2,1,0:T(8,128)S(1)} fusion(f32[64,5,128,128]{3,2,1,0:T(8,128)} %param.11, f32[64,5,16,128]{3,2,1,0:T(8,128)S(1)} %bitcast.333, pred[64,5]{1,0:T(8,128)(4,1)S(1)} %copy.306), kind=kOutput, calls=%fused_computation.84 | convolution fusion | flops 1007288320 | bytes 24117568 | tf_op jit(solution)/shard_map/nikc,ikrc->nir/dot_general | solution.py:48
  (175 shorter events, 34.8 us)
Async XLA Ops:
  6.5 30.0 %all-gather.2.cloned.1.call-start = ((), (), s32[]{:S(2)}) async-start(), calls=%async_computation | async-start | bytes 2359296 | tf_op jit(solution)/shard_map/all_gather | solution.py:33
  126.9 8.1 %collective-permute-start = (f32[16,384]{1,0:T(8,128)S(1)}, f32[16,384]{1,0:T(8,128)S(1)}, u32[]{:S(2)}, u32[]{:S(2)}) collective-permute-start(f32[16,384]{1,0:T(8,128)S(1)} %get-tuple-element.38), channel_id=1, source_target_pairs={{0,8},{8,16},{16,24},{24,32},{32,40},{40,48},{48,56},{56,64},{64,7... | collective-permute-start | bytes 73736 | tf_op jit(solution)/shard_map/ppermute | solution.py:20
  130.4 6.0 %collective-permute-start.1 = (f32[16,384]{1,0:T(8,128)S(1)}, f32[16,384]{1,0:T(8,128)S(1)}, u32[]{:S(2)}, u32[]{:S(2)}) collective-permute-start(f32[16,384]{1,0:T(8,128)S(1)} %get-tuple-element.39), channel_id=1, source_target_pairs={{8,0},{16,8},{24,16},{32,24},{40,32},{48,40},{56,48},{64,56},{72,6... | collective-permute-start | bytes 73736 | tf_op jit(solution)/shard_map/ppermute | solution.py:21
  162.4 8.5 %collective-permute-start.2 = (f32[16,384]{1,0:T(8,128)S(1)}, f32[16,384]{1,0:T(8,128)S(1)}, u32[]{:S(2)}, u32[]{:S(2)}) collective-permute-start(f32[16,384]{1,0:T(8,128)S(1)} %get-tuple-element.36), channel_id=1, source_target_pairs={{0,8},{8,16},{16,24},{24,32},{32,40},{40,48},{48,56},{56,64},{64,7... | collective-permute-start | bytes 73736 | tf_op jit(solution)/shard_map/ppermute | solution.py:20
  165.6 6.5 %collective-permute-start.3 = (f32[16,384]{1,0:T(8,128)S(1)}, f32[16,384]{1,0:T(8,128)S(1)}, u32[]{:S(2)}, u32[]{:S(2)}) collective-permute-start(f32[16,384]{1,0:T(8,128)S(1)} %get-tuple-element.37), channel_id=1, source_target_pairs={{8,0},{16,8},{24,16},{32,24},{40,32},{48,40},{56,48},{64,56},{72,6... | collective-permute-start | bytes 73736 | tf_op jit(solution)/shard_map/ppermute | solution.py:21
  197.3 8.3 %collective-permute-start.4 = (f32[16,384]{1,0:T(8,128)S(1)}, f32[16,384]{1,0:T(8,128)S(1)}, u32[]{:S(2)}, u32[]{:S(2)}) collective-permute-start(f32[16,384]{1,0:T(8,128)S(1)} %get-tuple-element.34), channel_id=1, source_target_pairs={{0,8},{8,16},{16,24},{24,32},{32,40},{40,48},{48,56},{56,64},{64,7... | collective-permute-start | bytes 73736 | tf_op jit(solution)/shard_map/ppermute | solution.py:20
  200.9 6.1 %collective-permute-start.5 = (f32[16,384]{1,0:T(8,128)S(1)}, f32[16,384]{1,0:T(8,128)S(1)}, u32[]{:S(2)}, u32[]{:S(2)}) collective-permute-start(f32[16,384]{1,0:T(8,128)S(1)} %get-tuple-element.35), channel_id=1, source_target_pairs={{8,0},{16,8},{24,16},{32,24},{40,32},{48,40},{56,48},{64,56},{72,6... | collective-permute-start | bytes 73736 | tf_op jit(solution)/shard_map/ppermute | solution.py:21
  209.0 23.2 %copy-start.21 = (f32[16,8192]{1,0:T(8,128)S(1)}, f32[16,8192]{1,0:T(8,128)}, u32[]{:S(2)}) copy-start(f32[16,8192]{1,0:T(8,128)} %copy-done.20) | copy-start | bytes 1572868
  209.0 23.2 %copy-start.30 = (f32[16,8192]{1,0:T(8,128)S(1)}, f32[16,8192]{1,0:T(8,128)}, u32[]{:S(2)}) copy-start(f32[16,8192]{1,0:T(8,128)} %get-tuple-element.15) | copy-start | bytes 1572868
  232.4 8.8 %collective-permute-start.6 = (f32[16,384]{1,0:T(8,128)S(1)}, f32[16,384]{1,0:T(8,128)S(1)}, u32[]{:S(2)}, u32[]{:S(2)}) collective-permute-start(f32[16,384]{1,0:T(8,128)S(1)} %get-tuple-element.32), channel_id=1, source_target_pairs={{0,8},{8,16},{16,24},{24,32},{32,40},{40,48},{48,56},{56,64},{64,7... | collective-permute-start | bytes 73736 | tf_op jit(solution)/shard_map/ppermute | solution.py:20
  236.0 6.1 %collective-permute-start.7 = (f32[16,384]{1,0:T(8,128)S(1)}, f32[16,384]{1,0:T(8,128)S(1)}, u32[]{:S(2)}, u32[]{:S(2)}) collective-permute-start(f32[16,384]{1,0:T(8,128)S(1)} %get-tuple-element.33), channel_id=1, source_target_pairs={{8,0},{16,8},{24,16},{32,24},{40,32},{48,40},{56,48},{64,56},{72,6... | collective-permute-start | bytes 73736 | tf_op jit(solution)/shard_map/ppermute | solution.py:21
  244.1 23.2 %copy-start.2 = (f32[2,16,8192]{2,1,0:T(8,128)S(1)}, f32[2,16,8192]{2,1,0:T(8,128)}, u32[]{:S(2)}) copy-start(f32[2,16,8192]{2,1,0:T(8,128)} %copy-done) | copy-start | bytes 3145732
  244.1 23.2 %copy-start.13 = (f32[64,2,8,128]{3,2,1,0:T(8,128)S(1)}, f32[64,2,8,128]{3,2,1,0:T(8,128)}, u32[]{:S(2)}) copy-start(f32[64,2,8,128]{3,2,1,0:T(8,128)} %copy-done.11) | copy-start | bytes 1572868
  244.1 23.2 %copy-start.22 = (f32[16,8192]{1,0:T(8,128)S(1)}, f32[16,8192]{1,0:T(8,128)}, u32[]{:S(2)}) copy-start(f32[16,8192]{1,0:T(8,128)} %copy-done.20) | copy-start | bytes 1572868
  244.1 23.2 %copy-start.31 = (f32[16,8192]{1,0:T(8,128)S(1)}, f32[16,8192]{1,0:T(8,128)}, u32[]{:S(2)}) copy-start(f32[16,8192]{1,0:T(8,128)} %get-tuple-element.15) | copy-start | bytes 1572868
  244.1 23.2 %copy-start.37 = (f32[64,2,8,128]{3,2,1,0:T(8,128)S(1)}, f32[64,2,8,128]{3,2,1,0:T(8,128)}, u32[]{:S(2)}) copy-start(f32[64,2,8,128]{3,2,1,0:T(8,128)} %copy-done.36) | copy-start | bytes 1572868
  267.6 8.3 %collective-permute-start.8 = (f32[16,384]{1,0:T(8,128)S(1)}, f32[16,384]{1,0:T(8,128)S(1)}, u32[]{:S(2)}, u32[]{:S(2)}) collective-permute-start(f32[16,384]{1,0:T(8,128)S(1)} %get-tuple-element.30), channel_id=1, source_target_pairs={{0,8},{8,16},{16,24},{24,32},{32,40},{40,48},{48,56},{56,64},{64,7... | collective-permute-start | bytes 73736 | tf_op jit(solution)/shard_map/ppermute | solution.py:20
  271.3 6.1 %collective-permute-start.9 = (f32[16,384]{1,0:T(8,128)S(1)}, f32[16,384]{1,0:T(8,128)S(1)}, u32[]{:S(2)}, u32[]{:S(2)}) collective-permute-start(f32[16,384]{1,0:T(8,128)S(1)} %get-tuple-element.31), channel_id=1, source_target_pairs={{8,0},{16,8},{24,16},{32,24},{40,32},{48,40},{56,48},{64,56},{72,6... | collective-permute-start | bytes 73736 | tf_op jit(solution)/shard_map/ppermute | solution.py:21
  303.4 8.4 %collective-permute-start.10 = (f32[16,384]{1,0:T(8,128)S(1)}, f32[16,384]{1,0:T(8,128)S(1)}, u32[]{:S(2)}, u32[]{:S(2)}) collective-permute-start(f32[16,384]{1,0:T(8,128)S(1)} %get-tuple-element.28), channel_id=1, source_target_pairs={{0,8},{8,16},{16,24},{24,32},{32,40},{40,48},{48,56},{56,64},{64,7... | collective-permute-start | bytes 73736 | tf_op jit(solution)/shard_map/ppermute | solution.py:20
  307.0 6.1 %collective-permute-start.11 = (f32[16,384]{1,0:T(8,128)S(1)}, f32[16,384]{1,0:T(8,128)S(1)}, u32[]{:S(2)}, u32[]{:S(2)}) collective-permute-start(f32[16,384]{1,0:T(8,128)S(1)} %get-tuple-element.29), channel_id=1, source_target_pairs={{8,0},{16,8},{24,16},{32,24},{40,32},{48,40},{56,48},{64,56},{72,6... | collective-permute-start | bytes 73736 | tf_op jit(solution)/shard_map/ppermute | solution.py:21
  338.3 8.3 %collective-permute-start.12 = (f32[16,384]{1,0:T(8,128)S(1)}, f32[16,384]{1,0:T(8,128)S(1)}, u32[]{:S(2)}, u32[]{:S(2)}) collective-permute-start(f32[16,384]{1,0:T(8,128)S(1)} %get-tuple-element.26), channel_id=1, source_target_pairs={{0,8},{8,16},{16,24},{24,32},{32,40},{40,48},{48,56},{56,64},{64,7... | collective-permute-start | bytes 73736 | tf_op jit(solution)/shard_map/ppermute | solution.py:20
  341.9 6.1 %collective-permute-start.13 = (f32[16,384]{1,0:T(8,128)S(1)}, f32[16,384]{1,0:T(8,128)S(1)}, u32[]{:S(2)}, u32[]{:S(2)}) collective-permute-start(f32[16,384]{1,0:T(8,128)S(1)} %get-tuple-element.27), channel_id=1, source_target_pairs={{8,0},{16,8},{24,16},{32,24},{40,32},{48,40},{56,48},{64,56},{72,6... | collective-permute-start | bytes 73736 | tf_op jit(solution)/shard_map/ppermute | solution.py:21
  350.0 23.2 %copy-start.18 = (f32[16,8192]{1,0:T(8,128)S(1)}, f32[16,8192]{1,0:T(8,128)}, u32[]{:S(2)}) copy-start(f32[16,8192]{1,0:T(8,128)} %copy-done.17) | copy-start | bytes 1572868
  350.0 23.2 %copy-start.27 = (f32[16,8192]{1,0:T(8,128)S(1)}, f32[16,8192]{1,0:T(8,128)}, u32[]{:S(2)}) copy-start(f32[16,8192]{1,0:T(8,128)} %get-tuple-element.13) | copy-start | bytes 1572868
  373.4 8.5 %collective-permute-start.14 = (f32[16,384]{1,0:T(8,128)S(1)}, f32[16,384]{1,0:T(8,128)S(1)}, u32[]{:S(2)}, u32[]{:S(2)}) collective-permute-start(f32[16,384]{1,0:T(8,128)S(1)} %get-tuple-element.24), channel_id=1, source_target_pairs={{0,8},{8,16},{16,24},{24,32},{32,40},{40,48},{48,56},{56,64},{64,7... | collective-permute-start | bytes 73736 | tf_op jit(solution)/shard_map/ppermute | solution.py:20
  377.0 6.1 %collective-permute-start.15 = (f32[16,384]{1,0:T(8,128)S(1)}, f32[16,384]{1,0:T(8,128)S(1)}, u32[]{:S(2)}, u32[]{:S(2)}) collective-permute-start(f32[16,384]{1,0:T(8,128)S(1)} %get-tuple-element.25), channel_id=1, source_target_pairs={{8,0},{16,8},{24,16},{32,24},{40,32},{48,40},{56,48},{64,56},{72,6... | collective-permute-start | bytes 73736 | tf_op jit(solution)/shard_map/ppermute | solution.py:21
  385.1 23.2 %copy-start.10 = (f32[64,2,8,128]{3,2,1,0:T(8,128)S(1)}, f32[64,2,8,128]{3,2,1,0:T(8,128)}, u32[]{:S(2)}) copy-start(f32[64,2,8,128]{3,2,1,0:T(8,128)} %copy-done.8) | copy-start | bytes 1572868
  385.1 23.2 %copy-start.19 = (f32[16,8192]{1,0:T(8,128)S(1)}, f32[16,8192]{1,0:T(8,128)}, u32[]{:S(2)}) copy-start(f32[16,8192]{1,0:T(8,128)} %copy-done.17) | copy-start | bytes 1572868
  385.1 23.2 %copy-start.28 = (f32[16,8192]{1,0:T(8,128)S(1)}, f32[16,8192]{1,0:T(8,128)}, u32[]{:S(2)}) copy-start(f32[16,8192]{1,0:T(8,128)} %get-tuple-element.13) | copy-start | bytes 1572868
  385.1 23.2 %copy-start.35 = (f32[64,2,8,128]{3,2,1,0:T(8,128)S(1)}, f32[64,2,8,128]{3,2,1,0:T(8,128)}, u32[]{:S(2)}) copy-start(f32[64,2,8,128]{3,2,1,0:T(8,128)} %copy-done.34) | copy-start | bytes 1572868
  385.1 23.2 %copy-start.41 = (f32[16,8192]{1,0:T(8,128)S(1)}, f32[16,8192]{1,0:T(8,128)}, u32[]{:S(2)}) copy-start(f32[16,8192]{1,0:T(8,128)} %copy-done.40) | copy-start | bytes 1572868
  408.6 8.3 %collective-permute-start.16 = (f32[16,384]{1,0:T(8,128)S(1)}, f32[16,384]{1,0:T(8,128)S(1)}, u32[]{:S(2)}, u32[]{:S(2)}) collective-permute-start(f32[16,384]{1,0:T(8,128)S(1)} %get-tuple-element.22), channel_id=1, source_target_pairs={{0,8},{8,16},{16,24},{24,32},{32,40},{40,48},{48,56},{56,64},{64,7... | collective-permute-start | bytes 73736 | tf_op jit(solution)/shard_map/ppermute | solution.py:20
  412.3 6.1 %collective-permute-start.17 = (f32[16,384]{1,0:T(8,128)S(1)}, f32[16,384]{1,0:T(8,128)S(1)}, u32[]{:S(2)}, u32[]{:S(2)}) collective-permute-start(f32[16,384]{1,0:T(8,128)S(1)} %get-tuple-element.23), channel_id=1, source_target_pairs={{8,0},{16,8},{24,16},{32,24},{40,32},{48,40},{56,48},{64,56},{72,6... | collective-permute-start | bytes 73736 | tf_op jit(solution)/shard_map/ppermute | solution.py:21
  444.4 8.7 %collective-permute-start.18 = (f32[16,384]{1,0:T(8,128)S(1)}, f32[16,384]{1,0:T(8,128)S(1)}, u32[]{:S(2)}, u32[]{:S(2)}) collective-permute-start(f32[16,384]{1,0:T(8,128)S(1)} %get-tuple-element.20), channel_id=1, source_target_pairs={{0,8},{8,16},{16,24},{24,32},{32,40},{40,48},{48,56},{56,64},{64,7... | collective-permute-start | bytes 73736 | tf_op jit(solution)/shard_map/ppermute | solution.py:20
  448.0 6.1 %collective-permute-start.19 = (f32[16,384]{1,0:T(8,128)S(1)}, f32[16,384]{1,0:T(8,128)S(1)}, u32[]{:S(2)}, u32[]{:S(2)}) collective-permute-start(f32[16,384]{1,0:T(8,128)S(1)} %get-tuple-element.21), channel_id=1, source_target_pairs={{8,0},{16,8},{24,16},{32,24},{40,32},{48,40},{56,48},{64,56},{72,6... | collective-permute-start | bytes 73736 | tf_op jit(solution)/shard_map/ppermute | solution.py:21
  456.1 31.5 %copy-start.42 = (s32[1,8]{1,0:T(1,128)S(1)}, s32[1,8]{1,0:T(1,128)}, u32[]{:S(2)}) copy-start(s32[1,8]{1,0:T(1,128)} %param.9) | copy-start | bytes 100
  456.1 31.5 %copy-start.44 = (s32[8,1]{0,1:T(1,128)S(1)}, s32[8,1]{0,1:T(1,128)}, u32[]{:S(2)}) copy-start(s32[8,1]{0,1:T(1,128)} %copy-done.43) | copy-start | bytes 100
  479.4 8.9 %collective-permute-start.20 = (f32[16,384]{1,0:T(8,128)S(1)}, f32[16,384]{1,0:T(8,128)S(1)}, u32[]{:S(2)}, u32[]{:S(2)}) collective-permute-start(f32[16,384]{1,0:T(8,128)S(1)} %get-tuple-element.18), channel_id=1, source_target_pairs={{0,8},{8,16},{16,24},{24,32},{32,40},{40,48},{48,56},{56,64},{64,7... | collective-permute-start | bytes 73736 | tf_op jit(solution)/shard_map/ppermute | solution.py:20
  483.0 6.1 %collective-permute-start.21 = (f32[16,384]{1,0:T(8,128)S(1)}, f32[16,384]{1,0:T(8,128)S(1)}, u32[]{:S(2)}, u32[]{:S(2)}) collective-permute-start(f32[16,384]{1,0:T(8,128)S(1)} %get-tuple-element.19), channel_id=1, source_target_pairs={{8,0},{16,8},{24,16},{32,24},{40,32},{48,40},{56,48},{64,56},{72,6... | collective-permute-start | bytes 73736 | tf_op jit(solution)/shard_map/ppermute | solution.py:21
  491.1 23.2 %copy-start.15 = (f32[16,8192]{1,0:T(8,128)S(1)}, f32[16,8192]{1,0:T(8,128)}, u32[]{:S(2)}) copy-start(f32[16,8192]{1,0:T(8,128)} %copy-done.14) | copy-start | bytes 1572868
  491.1 23.2 %copy-start.24 = (f32[16,8192]{1,0:T(8,128)S(1)}, f32[16,8192]{1,0:T(8,128)}, u32[]{:S(2)}) copy-start(f32[16,8192]{1,0:T(8,128)} %get-tuple-element.11) | copy-start | bytes 1572868
  515.1 10.8 %collective-permute-start.22 = (f32[16,384]{1,0:T(8,128)S(1)}, f32[16,384]{1,0:T(8,128)S(1)}, u32[]{:S(2)}, u32[]{:S(2)}) collective-permute-start(f32[16,384]{1,0:T(8,128)S(1)} %get-tuple-element.16), channel_id=1, source_target_pairs={{0,8},{8,16},{16,24},{24,32},{32,40},{40,48},{48,56},{56,64},{64,7... | collective-permute-start | bytes 73736 | tf_op jit(solution)/shard_map/ppermute | solution.py:20
  518.7 7.2 %collective-permute-start.23 = (f32[16,384]{1,0:T(8,128)S(1)}, f32[16,384]{1,0:T(8,128)S(1)}, u32[]{:S(2)}, u32[]{:S(2)}) collective-permute-start(f32[16,384]{1,0:T(8,128)S(1)} %get-tuple-element.17), channel_id=1, source_target_pairs={{8,0},{16,8},{24,16},{32,24},{40,32},{48,40},{56,48},{64,56},{72,6... | collective-permute-start | bytes 73736 | tf_op jit(solution)/shard_map/ppermute | solution.py:21
  527.9 23.2 %copy-start.7 = (f32[64,2,8,128]{3,2,1,0:T(8,128)S(1)}, f32[64,2,8,128]{3,2,1,0:T(8,128)}, u32[]{:S(2)}) copy-start(f32[64,2,8,128]{3,2,1,0:T(8,128)} %copy-done.5) | copy-start | bytes 1572868
  527.9 23.2 %copy-start.16 = (f32[16,8192]{1,0:T(8,128)S(1)}, f32[16,8192]{1,0:T(8,128)}, u32[]{:S(2)}) copy-start(f32[16,8192]{1,0:T(8,128)} %copy-done.14) | copy-start | bytes 1572868
  527.9 23.2 %copy-start.25 = (f32[16,8192]{1,0:T(8,128)S(1)}, f32[16,8192]{1,0:T(8,128)}, u32[]{:S(2)}) copy-start(f32[16,8192]{1,0:T(8,128)} %get-tuple-element.11) | copy-start | bytes 1572868
  527.9 23.2 %copy-start.33 = (f32[64,2,8,128]{3,2,1,0:T(8,128)S(1)}, f32[64,2,8,128]{3,2,1,0:T(8,128)}, u32[]{:S(2)}) copy-start(f32[64,2,8,128]{3,2,1,0:T(8,128)} %copy-done.32) | copy-start | bytes 1572868
  527.9 23.2 %copy-start.39 = (f32[16,8192]{1,0:T(8,128)S(1)}, f32[16,8192]{1,0:T(8,128)}, u32[]{:S(2)}) copy-start(f32[16,8192]{1,0:T(8,128)} %copy-done.38) | copy-start | bytes 1572868
  (22 other events, 312.8 us)
Sparse Core Ops, SparseCore 0:
  9.0 27.4 all-gather.1
where the time goes:
time: 566 us; the launch traced here: 559 us
  matrix products  277 us (49%)
  local copies, waits for them, and re-layouts  115 us (20%)
  starting transfers between devices  100 us (18%)
  waiting for transfers between devices  38.7 us (7%)
  between operations  16.6 us (3%)
  other arithmetic  11.6 us (2%)
    dot_general x12, matrix products, operate(): jnp.einsum('nikc,ikrc->nir', picked, blocks, precision=lax.Precision.HIGH...  277 us
    gather x2, local copies, waits for them, and re-layouts, on_device(): owned = jnp.take(gathered, source, axis=2)  71.6 us
    ppermute x12, starting transfers between devices, padded_2(): after = lax.ppermute(initial, axis, down)  57.6 us
    ppermute x12, starting transfers between devices, padded_2(): before = lax.ppermute(last, axis, up)  42.8 us
    all_gather x1, waiting for transfers between devices, on_device(): gathered = lax.all_gather(stacked, 'fold', axis=2, tiled=True)  24.7 us
    gather x12, local copies, waits for them, and re-layouts, operate(): picked = jnp.take(extended, columns, axis=1)  22.7 us
    all_gather x1, local copies, waits for them, and re-layouts, on_device(): gathered = lax.all_gather(stacked, 'fold', axis=2, tiled=True)  18.6 us
    ppermute x12, waiting for transfers between devices, padded_2(): after = lax.ppermute(initial, axis, down)  14 us
  transfers between devices with their start and end apart: 25, of which 12 were waited for; matrix products, arithmetic and copies ran while one was open for 1% of the time, Pallas kernels for 0%

commit v1 on v0

--- a/solution.py
+++ b/solution.py
@@ -8,6 +8,12 @@
 DEGREE = 4
 upper_bound = 4.5
 lower_bound = 1.35
+
+
+def joined_along(pieces, dim):
+    pieces = jnp.moveaxis(pieces, 0, dim)
+    shape = pieces.shape
+    return pieces.reshape(*shape[:dim], shape[dim] * shape[dim + 1], *shape[dim + 2 :])
 
 
 def padded_2(shard, sides, width):
@@ -30,7 +36,19 @@
     live_rows = counts[0]
     starts = jnp.cumsum(live_rows) - live_rows
     stacked = jnp.stack([right_side, initial])
-    gathered = lax.all_gather(stacked, "fold", axis=2, tiled=True)
+    size = lax.axis_size("fold")
+    pairs = [(i_2, (i_2 + 1) % size) for i_2 in range(size)]
+    back = [(b, a) for a, b in pairs]
+    lower, upper = ([], [])
+    for step_2 in range(size - 1):
+        if step_2 % 2 == 0:
+            lower.append(lax.ppermute(lower[-1] if lower else stacked, "fold", pairs))
+        else:
+            upper.append(lax.ppermute(upper[-1] if upper else stacked, "fold", back))
+    pieces = jnp.stack([*lower[::-1], stacked, *upper])
+    shift = lax.axis_index("fold") - len(lower)
+    pieces = pieces[(jnp.arange(size) - shift) % size]
+    gathered = joined_along(pieces, 2)
     position = lax.axis_index("fold")
     row_ids = jnp.arange(own_blocks * width, dtype=jnp.int32)
     covered = starts[None, :] <= row_ids[:, None]

time: 566 us -> 560 us (0.989)
  between operations: 16.6 us -> 3.39 us
  starting transfers between devices: 100 us -> 108 us
  waiting for transfers between devices: 38.7 us -> 32.1 us
    all_gather x1 -> x0, waiting for transfers between devices: 24.7 us -> none  [on_device(): gathered = lax.all_gather(stacked, 'fold', axis=2, tiled=True)]
    all_gather x1 -> x0, local copies, waits for them, and re-layouts: 18.6 us -> none  [on_device(): gathered = lax.all_gather(stacked, 'fold', axis=2, tiled=True)]
    ppermute x0 -> x7, waiting for transfers between devices: none -> 18 us  [the longest x4 18 us: on_device(): lower.append(lax.ppermute(lower[-1] if lower else stacked, 'fold', pairs))]
    reshape x0 -> x1, local copies, waits for them, and re-layouts: none -> 16.6 us  [joined_along(): pieces.reshape(*shape[:dim], shape[dim] * shape[dim + 1], *shape[dim + 2:])]
    ppermute x0 -> x7, starting transfers between devices: none -> 8.14 us  [the longest x3 8.13 us: on_device(): upper.append(lax.ppermute(upper[-1] if upper else stacked, 'fold', back))]
  transfers between devices with their start and end apart: 25 -> 31, of which waited for: 12 -> 15; matrix products, arithmetic and copies ran while one was open for 1% -> 2% of each run, Pallas kernels for 0% -> 0%
where the time goes in v1:
time: 560 us; the launch traced here: 554 us
  matrix products  278 us (50%)
  local copies, waits for them, and re-layouts  120 us (21%)
  starting transfers between devices  108 us (19%)
  waiting for transfers between devices  32.1 us (6%)
  other arithmetic  11.7 us (2%)
    dot_general x12, matrix products, operate(): jnp.einsum('nikc,ikrc->nir', picked, blocks, precision=lax.Precision.HIGH...  278 us
    gather x2, local copies, waits for them, and re-layouts, on_device(): owned = jnp.take(gathered, source, axis=2)  71.7 us
    ppermute x12, starting transfers between devices, padded_2(): after = lax.ppermute(initial, axis, down)  55.3 us
    ppermute x12, starting transfers between devices, padded_2(): before = lax.ppermute(last, axis, up)  45 us
    gather x12, local copies, waits for them, and re-layouts, operate(): picked = jnp.take(extended, columns, axis=1)  22.7 us
    ppermute x4, waiting for transfers between devices, on_device(): lower.append(lax.ppermute(lower[-1] if lower else stacked, 'fold', pairs))  18 us
    reshape x1, local copies, waits for them, and re-layouts, joined_along(): pieces.reshape(*shape[:dim], shape[dim] * shape[dim + 1], *shape[dim + 2:])  16.6 us
    ppermute x12, waiting for transfers between devices, padded_2(): after = lax.ppermute(initial, axis, down)  14 us
  transfers between devices with their start and end apart: 31, of which 15 were waited for; matrix products, arithmetic and copies ran while one was open for 2% of the time, Pallas kernels for 0%

profile of v1, /device:TPU:8, one launch (start us, length us, event | category | flops | bytes accessed | tf_op | source)
XLA Modules:
  0.0 553.8 jit_solution(13589345400071892902)
XLA Ops:
  1.0 2.2 collective-permute-start.4
  5.6 4.6 collective-permute-done
  11.6 5.6 %collective-permute-done.1 = f32[2,16,2048]{2,1,0:T(8,128)S(1)} collective-permute-done((f32[2,16,2048]{2,1,0:T(8,128)S(1)}, f32[2,16,2048]{2,1,0:T(8,128)S(1)}, u32[]{:S(2)}, u32[]{:S(2)}) %collective-permute-start.1) | collective-permute-done | bytes 262176 | tf_op jit(solution)/shard_map/ppermute | solution.py:45
  17.3 3.0 collective-permute-start.5
  20.3 4.0 collective-permute-done.2
  24.6 3.0 collective-permute-start.6
  27.5 3.8 collective-permute-done.3
  37.2 2.3 gather_fusion
  39.5 16.6 %copy.369 = f32[2,16,8,2048]{1,0,3,2:T(2,128)} copy(f32[2,16,8,2048]{3,1,0,2:T(8,128)S(1)} %bitcast.366) | data formatting | bytes 4194304 | tf_op jit(solution)/shard_map/reshape | solution.py:16
  56.1 62.4 %gather_fusion.1 = f32[8192,2,16]{2,1,0:T(2,128)} fusion(f32[2,16,16384]{1,0,2:T(2,128)} %bitcast.365, s32[8192]{0:T(1024)S(1)} %broadcast_clamp_fusion), kind=kCustom, calls=%fused_computation.13 | custom fusion | bytes 2129920 | tf_op jit(solution)/shard_map/jit(_take)/gather | solution.py:58
  118.4 9.3 %copy.308 = f32[8192,2,16]{0,2,1:T(8,128)S(1)} copy(f32[8192,2,16]{2,1,0:T(2,128)} %gather_fusion.1) | data formatting | bytes 2097152 | tf_op jit(solution)/shard_map/jit(_take)/gather | solution.py:58
  127.9 3.8 collective-permute-start.7
  131.8 4.1 collective-permute-start.8
  139.4 23.1 %fusion.60 = f32[64,2,8,128]{3,2,1,0:T(8,128)S(1)} fusion(f32[64,5,128,128]{3,2,1,0:T(8,128)} %param.11, f32[64,5,16,128]{3,2,1,0:T(8,128)S(1)} %bitcast.354, pred[64,5]{1,0:T(8,128)(4,1)S(1)} %copy.309), kind=kOutput, calls=%fused_computation.74 | convolution fusion | flops 1007288320 | bytes 24117568 | tf_op jit(solution)/shard_map/nikc,ikrc->nir/dot_general | solution.py:66
  163.5 3.8 collective-permute-start.9
  167.3 4.6 collective-permute-start.10
  175.1 23.1 %fusion.63 = f32[64,2,8,128]{3,2,1,0:T(8,128)S(1)} fusion(f32[64,5,128,128]{3,2,1,0:T(8,128)} %param.11, f32[64,5,16,128]{3,2,1,0:T(8,128)S(1)} %bitcast.355, pred[64,5]{1,0:T(8,128)(4,1)S(1)} %copy.309), kind=kOutput, calls=%fused_computation.75 | convolution fusion | flops 1007288320 | bytes 24117568 | tf_op jit(solution)/shard_map/nikc,ikrc->nir/dot_general | solution.py:66
  198.4 3.7 collective-permute-start.11
  202.1 4.5 collective-permute-start.12
  210.1 23.1 %fusion.66 = f32[64,2,8,128]{3,2,1,0:T(8,128)S(1)} fusion(f32[64,5,128,128]{3,2,1,0:T(8,128)} %param.11, f32[64,5,16,128]{3,2,1,0:T(8,128)S(1)} %bitcast.356, pred[64,5]{1,0:T(8,128)(4,1)S(1)} %copy.309), kind=kOutput, calls=%fused_computation.76 | convolution fusion | flops 1007288320 | bytes 24117568 | tf_op jit(solution)/shard_map/nikc,ikrc->nir/dot_general | solution.py:66
  233.4 3.7 collective-permute-start.13
  237.2 5.0 collective-permute-start.14
  245.2 23.2 %fusion.69 = f32[64,2,8,128]{3,2,1,0:T(8,128)S(1)} fusion(f32[64,5,128,128]{3,2,1,0:T(8,128)} %param.11, f32[64,5,16,128]{3,2,1,0:T(8,128)S(1)} %bitcast.357, pred[64,5]{1,0:T(8,128)(4,1)S(1)} %copy.309), kind=kOutput, calls=%fused_computation.77 | convolution fusion | flops 1007288320 | bytes 24117568 | tf_op jit(solution)/shard_map/nikc,ikrc->nir/dot_general | solution.py:66
  268.8 3.7 collective-permute-start.15
  272.5 4.5 collective-permute-start.16
  280.5 23.1 %fusion.72 = f32[64,2,8,128]{3,2,1,0:T(8,128)S(1)} fusion(f32[64,5,128,128]{3,2,1,0:T(8,128)} %param.11, f32[64,5,16,128]{3,2,1,0:T(8,128)S(1)} %bitcast.358, pred[64,5]{1,0:T(8,128)(4,1)S(1)} %copy.309), kind=kOutput, calls=%fused_computation.78 | convolution fusion | flops 1007288320 | bytes 24117568 | tf_op jit(solution)/shard_map/nikc,ikrc->nir/dot_general | solution.py:66
  304.5 3.7 collective-permute-start.17
  308.3 4.7 collective-permute-start.18
  316.2 23.1 %fusion.75 = f32[64,2,8,128]{3,2,1,0:T(8,128)S(1)} fusion(f32[64,5,128,128]{3,2,1,0:T(8,128)} %param.11, f32[64,5,16,128]{3,2,1,0:T(8,128)S(1)} %bitcast.359, pred[64,5]{1,0:T(8,128)(4,1)S(1)} %copy.309), kind=kOutput, calls=%fused_computation.79 | convolution fusion | flops 1007288320 | bytes 24117568 | tf_op jit(solution)/shard_map/nikc,ikrc->nir/dot_general | solution.py:66
  339.5 3.7 collective-permute-start.19
  343.2 4.5 collective-permute-start.20
  349.3 1.9 gather_fusion.8
  351.2 23.1 %fusion.78 = f32[64,2,8,128]{3,2,1,0:T(8,128)S(1)} fusion(f32[64,5,128,128]{3,2,1,0:T(8,128)} %param.11, f32[64,5,16,128]{3,2,1,0:T(8,128)S(1)} %bitcast.360, pred[64,5]{1,0:T(8,128)(4,1)S(1)} %copy.309), kind=kOutput, calls=%fused_computation.80 | convolution fusion | flops 1007288320 | bytes 24117568 | tf_op jit(solution)/shard_map/nikc,ikrc->nir/dot_general | solution.py:66
  374.6 3.7 collective-permute-start.21
  378.3 4.7 collective-permute-start.22
  386.3 23.2 %fusion.81 = f32[64,2,8,128]{3,2,1,0:T(8,128)S(1)} fusion(f32[64,5,128,128]{3,2,1,0:T(8,128)} %param.11, f32[64,5,16,128]{3,2,1,0:T(8,128)S(1)} %bitcast.361, pred[64,5]{1,0:T(8,128)(4,1)S(1)} %copy.309), kind=kOutput, calls=%fused_computation.81 | convolution fusion | flops 1007288320 | bytes 24117568 | tf_op jit(solution)/shard_map/nikc,ikrc->nir/dot_general | solution.py:66
  409.9 3.7 collective-permute-start.23
  413.6 4.5 collective-permute-start.24
  421.6 23.1 %fusion.84 = f32[64,2,8,128]{3,2,1,0:T(8,128)S(1)} fusion(f32[64,5,128,128]{3,2,1,0:T(8,128)} %param.11, f32[64,5,16,128]{3,2,1,0:T(8,128)S(1)} %bitcast.362, pred[64,5]{1,0:T(8,128)(4,1)S(1)} %copy.309), kind=kOutput, calls=%fused_computation.82 | convolution fusion | flops 1007288320 | bytes 24117568 | tf_op jit(solution)/shard_map/nikc,ikrc->nir/dot_general | solution.py:66
  445.7 3.7 collective-permute-start.25
  449.4 4.9 collective-permute-start.26
  457.4 23.1 %fusion.87 = f32[64,2,8,128]{3,2,1,0:T(8,128)S(1)} fusion(f32[64,5,128,128]{3,2,1,0:T(8,128)} %param.11, f32[64,5,16,128]{3,2,1,0:T(8,128)S(1)} %bitcast.363, pred[64,5]{1,0:T(8,128)(4,1)S(1)} %copy.309), kind=kOutput, calls=%fused_computation.83 | convolution fusion | flops 1007288320 | bytes 24117568 | tf_op jit(solution)/shard_map/nikc,ikrc->nir/dot_general | solution.py:66
  480.6 3.7 collective-permute-start.27
  484.4 4.5 collective-permute-start.28
  492.4 23.1 %fusion.90 = f32[64,2,8,128]{3,2,1,0:T(8,128)S(1)} fusion(f32[64,5,128,128]{3,2,1,0:T(8,128)} %param.11, f32[64,5,16,128]{3,2,1,0:T(8,128)S(1)} %bitcast.364, pred[64,5]{1,0:T(8,128)(4,1)S(1)} %copy.309), kind=kOutput, calls=%fused_computation.84 | convolution fusion | flops 1007288320 | bytes 24117568 | tf_op jit(solution)/shard_map/nikc,ikrc->nir/dot_general | solution.py:66
  516.4 3.7 collective-permute-start.29
  520.1 4.7 collective-permute-start.30
  529.3 23.2 %fusion.93 = f32[64,2,8,128]{3,2,1,0:T(8,128)S(1)} fusion(f32[64,5,128,128]{3,2,1,0:T(8,128)} %param.11, f32[64,5,16,128]{3,2,1,0:T(8,128)S(1)} %bitcast.353, pred[64,5]{1,0:T(8,128)(4,1)S(1)} %copy.309), kind=kOutput, calls=%fused_computation.85 | convolution fusion | flops 1007288320 | bytes 24117568 | tf_op jit(solution)/shard_map/nikc,ikrc->nir/dot_general | solution.py:66
  (201 shorter events, 53.9 us)
Async XLA Ops:
  0.0 34.2 %copy-start.42 = (f32[16,2048]{1,0:T(8,128)S(1)}, f32[16,2048]{1,0:T(8,128)}, u32[]{:S(2)}) copy-start(f32[16,2048]{1,0:T(8,128)} %param.8) | copy-start | bytes 393220
  0.0 34.2 %copy-start.43 = (f32[16,2048]{1,0:T(8,128)S(1)}, f32[16,2048]{1,0:T(8,128)}, u32[]{:S(2)}) copy-start(f32[16,2048]{1,0:T(8,128)} %param.7) | copy-start | bytes 393220
  1.0 16.3 %collective-permute-start.4 = (f32[2,16,2048]{2,1,0:T(8,128)S(1)}, f32[2,16,2048]{2,1,0:T(8,128)S(1)}, u32[]{:S(2)}, u32[]{:S(2)}) collective-permute-start(f32[2,16,2048]{2,1,0:T(8,128)S(1)} %pad_maximum_fusion), channel_id=1, source_target_pairs={{1,0},{2,1},{3,2},{4,3},{5,4},{6,5},{7,6},{0,7},{9,8},{10,9},{11,1... | collective-permute-start | bytes 786440 | tf_op jit(solution)/shard_map/ppermute | solution.py:47
  3.2 7.0 %collective-permute-start = (f32[2,16,2048]{2,1,0:T(8,128)S(1)}, f32[2,16,2048]{2,1,0:T(8,128)S(1)}, u32[]{:S(2)}, u32[]{:S(2)}) collective-permute-start(f32[2,16,2048]{2,1,0:T(8,128)S(1)} %pad_maximum_fusion), channel_id=1, source_target_pairs={{0,1},{1,2},{2,3},{3,4},{4,5},{5,6},{6,7},{7,0},{8,9},{9,10},{10,1... | collective-permute-start | bytes 786440 | tf_op jit(solution)/shard_map/ppermute | solution.py:45
  10.3 7.0 %collective-permute-start.1 = (f32[2,16,2048]{2,1,0:T(8,128)S(1)}, f32[2,16,2048]{2,1,0:T(8,128)S(1)}, u32[]{:S(2)}, u32[]{:S(2)}) collective-permute-start(f32[2,16,2048]{2,1,0:T(8,128)S(1)} %collective-permute-done), channel_id=1, source_target_pairs={{0,1},{1,2},{2,3},{3,4},{4,5},{5,6},{6,7},{7,0},{8,9},{9,10},{10,1... | collective-permute-start | bytes 786440 | tf_op jit(solution)/shard_map/ppermute | solution.py:45
  17.3 7.0 %collective-permute-start.2 = (f32[2,16,2048]{2,1,0:T(8,128)S(1)}, f32[2,16,2048]{2,1,0:T(8,128)S(1)}, u32[]{:S(2)}, u32[]{:S(2)}) collective-permute-start(f32[2,16,2048]{2,1,0:T(8,128)S(1)} %collective-permute-done.1), channel_id=1, source_target_pairs={{0,1},{1,2},{2,3},{3,4},{4,5},{5,6},{6,7},{7,0},{8,9},{9,10},{10,1... | collective-permute-start | bytes 786440 | tf_op jit(solution)/shard_map/ppermute | solution.py:45
  17.3 7.2 %collective-permute-start.5 = (f32[2,16,2048]{2,1,0:T(8,128)S(1)}, f32[2,16,2048]{2,1,0:T(8,128)S(1)}, u32[]{:S(2)}, u32[]{:S(2)}) collective-permute-start(f32[2,16,2048]{2,1,0:T(8,128)S(1)} %collective-permute-done.4), channel_id=1, source_target_pairs={{1,0},{2,1},{3,2},{4,3},{5,4},{6,5},{7,6},{0,7},{9,8},{10,9},{11,1... | collective-permute-start | bytes 786440 | tf_op jit(solution)/shard_map/ppermute | solution.py:47
  24.3 7.0 %collective-permute-start.3 = (f32[2,16,2048]{2,1,0:T(8,128)S(1)}, f32[2,16,2048]{2,1,0:T(8,128)S(1)}, u32[]{:S(2)}, u32[]{:S(2)}) collective-permute-start(f32[2,16,2048]{2,1,0:T(8,128)S(1)} %collective-permute-done.2), channel_id=1, source_target_pairs={{0,1},{1,2},{2,3},{3,4},{4,5},{5,6},{6,7},{7,0},{8,9},{9,10},{10,1... | collective-permute-start | bytes 786440 | tf_op jit(solution)/shard_map/ppermute | solution.py:45
  24.6 11.9 %collective-permute-start.6 = (f32[2,16,2048]{2,1,0:T(8,128)S(1)}, f32[2,16,2048]{2,1,0:T(8,128)S(1)}, u32[]{:S(2)}, u32[]{:S(2)}) collective-permute-start(f32[2,16,2048]{2,1,0:T(8,128)S(1)} %collective-permute-done.5), channel_id=1, source_target_pairs={{1,0},{2,1},{3,2},{4,3},{5,4},{6,5},{7,6},{0,7},{9,8},{10,9},{11,1... | collective-permute-start | bytes 786440 | tf_op jit(solution)/shard_map/ppermute | solution.py:47
  127.9 8.1 %collective-permute-start.7 = (f32[16,384]{1,0:T(8,128)S(1)}, f32[16,384]{1,0:T(8,128)S(1)}, u32[]{:S(2)}, u32[]{:S(2)}) collective-permute-start(f32[16,384]{1,0:T(8,128)S(1)} %get-tuple-element.38), channel_id=1, source_target_pairs={{0,8},{8,16},{16,24},{24,32},{32,40},{40,48},{48,56},{56,64},{64,7... | collective-permute-start | bytes 73736 | tf_op jit(solution)/shard_map/ppermute | solution.py:26
  131.8 5.7 %collective-permute-start.8 = (f32[16,384]{1,0:T(8,128)S(1)}, f32[16,384]{1,0:T(8,128)S(1)}, u32[]{:S(2)}, u32[]{:S(2)}) collective-permute-start(f32[16,384]{1,0:T(8,128)S(1)} %get-tuple-element.39), channel_id=1, source_target_pairs={{8,0},{16,8},{24,16},{32,24},{40,32},{48,40},{56,48},{64,56},{72,6... | collective-permute-start | bytes 73736 | tf_op jit(solution)/shard_map/ppermute | solution.py:27
  163.5 8.5 %collective-permute-start.9 = (f32[16,384]{1,0:T(8,128)S(1)}, f32[16,384]{1,0:T(8,128)S(1)}, u32[]{:S(2)}, u32[]{:S(2)}) collective-permute-start(f32[16,384]{1,0:T(8,128)S(1)} %get-tuple-element.36), channel_id=1, source_target_pairs={{0,8},{8,16},{16,24},{24,32},{32,40},{40,48},{48,56},{56,64},{64,7... | collective-permute-start | bytes 73736 | tf_op jit(solution)/shard_map/ppermute | solution.py:26
  167.3 5.8 %collective-permute-start.10 = (f32[16,384]{1,0:T(8,128)S(1)}, f32[16,384]{1,0:T(8,128)S(1)}, u32[]{:S(2)}, u32[]{:S(2)}) collective-permute-start(f32[16,384]{1,0:T(8,128)S(1)} %get-tuple-element.37), channel_id=1, source_target_pairs={{8,0},{16,8},{24,16},{32,24},{40,32},{48,40},{56,48},{64,56},{72,6... | collective-permute-start | bytes 73736 | tf_op jit(solution)/shard_map/ppermute | solution.py:27
  198.4 8.3 %collective-permute-start.11 = (f32[16,384]{1,0:T(8,128)S(1)}, f32[16,384]{1,0:T(8,128)S(1)}, u32[]{:S(2)}, u32[]{:S(2)}) collective-permute-start(f32[16,384]{1,0:T(8,128)S(1)} %get-tuple-element.34), channel_id=1, source_target_pairs={{0,8},{8,16},{16,24},{24,32},{32,40},{40,48},{48,56},{56,64},{64,7... | collective-permute-start | bytes 73736 | tf_op jit(solution)/shard_map/ppermute | solution.py:26
  202.1 6.0 %collective-permute-start.12 = (f32[16,384]{1,0:T(8,128)S(1)}, f32[16,384]{1,0:T(8,128)S(1)}, u32[]{:S(2)}, u32[]{:S(2)}) collective-permute-start(f32[16,384]{1,0:T(8,128)S(1)} %get-tuple-element.35), channel_id=1, source_target_pairs={{8,0},{16,8},{24,16},{32,24},{40,32},{48,40},{56,48},{64,56},{72,6... | collective-permute-start | bytes 73736 | tf_op jit(solution)/shard_map/ppermute | solution.py:27
  233.4 8.8 %collective-permute-start.13 = (f32[16,384]{1,0:T(8,128)S(1)}, f32[16,384]{1,0:T(8,128)S(1)}, u32[]{:S(2)}, u32[]{:S(2)}) collective-permute-start(f32[16,384]{1,0:T(8,128)S(1)} %get-tuple-element.32), channel_id=1, source_target_pairs={{0,8},{8,16},{16,24},{24,32},{32,40},{40,48},{48,56},{56,64},{64,7... | collective-permute-start | bytes 73736 | tf_op jit(solution)/shard_map/ppermute | solution.py:26
  237.2 6.0 %collective-permute-start.14 = (f32[16,384]{1,0:T(8,128)S(1)}, f32[16,384]{1,0:T(8,128)S(1)}, u32[]{:S(2)}, u32[]{:S(2)}) collective-permute-start(f32[16,384]{1,0:T(8,128)S(1)} %get-tuple-element.33), channel_id=1, source_target_pairs={{8,0},{16,8},{24,16},{32,24},{40,32},{48,40},{56,48},{64,56},{72,6... | collective-permute-start | bytes 73736 | tf_op jit(solution)/shard_map/ppermute | solution.py:27
  245.2 23.3 %copy-start.13 = (f32[64,2,8,128]{3,2,1,0:T(8,128)S(1)}, f32[64,2,8,128]{3,2,1,0:T(8,128)}, u32[]{:S(2)}) copy-start(f32[64,2,8,128]{3,2,1,0:T(8,128)} %copy-done.11) | copy-start | bytes 1572868
  245.2 23.3 %copy-start.22 = (f32[16,8192]{1,0:T(8,128)S(1)}, f32[16,8192]{1,0:T(8,128)}, u32[]{:S(2)}) copy-start(f32[16,8192]{1,0:T(8,128)} %copy-done.20) | copy-start | bytes 1572868
  245.2 23.3 %copy-start.31 = (f32[16,8192]{1,0:T(8,128)S(1)}, f32[16,8192]{1,0:T(8,128)}, u32[]{:S(2)}) copy-start(f32[16,8192]{1,0:T(8,128)} %get-tuple-element.15) | copy-start | bytes 1572868
  245.2 23.3 %copy-start.37 = (f32[64,2,8,128]{3,2,1,0:T(8,128)S(1)}, f32[64,2,8,128]{3,2,1,0:T(8,128)}, u32[]{:S(2)}) copy-start(f32[64,2,8,128]{3,2,1,0:T(8,128)} %copy-done.36) | copy-start | bytes 1572868
  268.8 8.3 %collective-permute-start.15 = (f32[16,384]{1,0:T(8,128)S(1)}, f32[16,384]{1,0:T(8,128)S(1)}, u32[]{:S(2)}, u32[]{:S(2)}) collective-permute-start(f32[16,384]{1,0:T(8,128)S(1)} %get-tuple-element.30), channel_id=1, source_target_pairs={{0,8},{8,16},{16,24},{24,32},{32,40},{40,48},{48,56},{56,64},{64,7... | collective-permute-start | bytes 73736 | tf_op jit(solution)/shard_map/ppermute | solution.py:26
  272.5 6.0 %collective-permute-start.16 = (f32[16,384]{1,0:T(8,128)S(1)}, f32[16,384]{1,0:T(8,128)S(1)}, u32[]{:S(2)}, u32[]{:S(2)}) collective-permute-start(f32[16,384]{1,0:T(8,128)S(1)} %get-tuple-element.31), channel_id=1, source_target_pairs={{8,0},{16,8},{24,16},{32,24},{40,32},{48,40},{56,48},{64,56},{72,6... | collective-permute-start | bytes 73736 | tf_op jit(solution)/shard_map/ppermute | solution.py:27
  304.5 8.4 %collective-permute-start.17 = (f32[16,384]{1,0:T(8,128)S(1)}, f32[16,384]{1,0:T(8,128)S(1)}, u32[]{:S(2)}, u32[]{:S(2)}) collective-permute-start(f32[16,384]{1,0:T(8,128)S(1)} %get-tuple-element.28), channel_id=1, source_target_pairs={{0,8},{8,16},{16,24},{24,32},{32,40},{40,48},{48,56},{56,64},{64,7... | collective-permute-start | bytes 73736 | tf_op jit(solution)/shard_map/ppermute | solution.py:26
  308.3 6.0 %collective-permute-start.18 = (f32[16,384]{1,0:T(8,128)S(1)}, f32[16,384]{1,0:T(8,128)S(1)}, u32[]{:S(2)}, u32[]{:S(2)}) collective-permute-start(f32[16,384]{1,0:T(8,128)S(1)} %get-tuple-element.29), channel_id=1, source_target_pairs={{8,0},{16,8},{24,16},{32,24},{40,32},{48,40},{56,48},{64,56},{72,6... | collective-permute-start | bytes 73736 | tf_op jit(solution)/shard_map/ppermute | solution.py:27
  339.5 8.3 %collective-permute-start.19 = (f32[16,384]{1,0:T(8,128)S(1)}, f32[16,384]{1,0:T(8,128)S(1)}, u32[]{:S(2)}, u32[]{:S(2)}) collective-permute-start(f32[16,384]{1,0:T(8,128)S(1)} %get-tuple-element.26), channel_id=1, source_target_pairs={{0,8},{8,16},{16,24},{24,32},{32,40},{40,48},{48,56},{56,64},{64,7... | collective-permute-start | bytes 73736 | tf_op jit(solution)/shard_map/ppermute | solution.py:26
  343.2 6.0 %collective-permute-start.20 = (f32[16,384]{1,0:T(8,128)S(1)}, f32[16,384]{1,0:T(8,128)S(1)}, u32[]{:S(2)}, u32[]{:S(2)}) collective-permute-start(f32[16,384]{1,0:T(8,128)S(1)} %get-tuple-element.27), channel_id=1, source_target_pairs={{8,0},{16,8},{24,16},{32,24},{40,32},{48,40},{56,48},{64,56},{72,6... | collective-permute-start | bytes 73736 | tf_op jit(solution)/shard_map/ppermute | solution.py:27
  374.6 8.5 %collective-permute-start.21 = (f32[16,384]{1,0:T(8,128)S(1)}, f32[16,384]{1,0:T(8,128)S(1)}, u32[]{:S(2)}, u32[]{:S(2)}) collective-permute-start(f32[16,384]{1,0:T(8,128)S(1)} %get-tuple-element.24), channel_id=1, source_target_pairs={{0,8},{8,16},{16,24},{24,32},{32,40},{40,48},{48,56},{56,64},{64,7... | collective-permute-start | bytes 73736 | tf_op jit(solution)/shard_map/ppermute | solution.py:26
  378.3 6.0 %collective-permute-start.22 = (f32[16,384]{1,0:T(8,128)S(1)}, f32[16,384]{1,0:T(8,128)S(1)}, u32[]{:S(2)}, u32[]{:S(2)}) collective-permute-start(f32[16,384]{1,0:T(8,128)S(1)} %get-tuple-element.25), channel_id=1, source_target_pairs={{8,0},{16,8},{24,16},{32,24},{40,32},{48,40},{56,48},{64,56},{72,6... | collective-permute-start | bytes 73736 | tf_op jit(solution)/shard_map/ppermute | solution.py:27
  386.3 23.3 %copy-start.10 = (f32[64,2,8,128]{3,2,1,0:T(8,128)S(1)}, f32[64,2,8,128]{3,2,1,0:T(8,128)}, u32[]{:S(2)}) copy-start(f32[64,2,8,128]{3,2,1,0:T(8,128)} %copy-done.8) | copy-start | bytes 1572868
  386.3 23.3 %copy-start.19 = (f32[16,8192]{1,0:T(8,128)S(1)}, f32[16,8192]{1,0:T(8,128)}, u32[]{:S(2)}) copy-start(f32[16,8192]{1,0:T(8,128)} %copy-done.17) | copy-start | bytes 1572868
  386.3 23.3 %copy-start.28 = (f32[16,8192]{1,0:T(8,128)S(1)}, f32[16,8192]{1,0:T(8,128)}, u32[]{:S(2)}) copy-start(f32[16,8192]{1,0:T(8,128)} %get-tuple-element.13) | copy-start | bytes 1572868
  386.3 23.3 %copy-start.35 = (f32[64,2,8,128]{3,2,1,0:T(8,128)S(1)}, f32[64,2,8,128]{3,2,1,0:T(8,128)}, u32[]{:S(2)}) copy-start(f32[64,2,8,128]{3,2,1,0:T(8,128)} %copy-done.34) | copy-start | bytes 1572868
  386.3 23.3 %copy-start.41 = (f32[16,8192]{1,0:T(8,128)S(1)}, f32[16,8192]{1,0:T(8,128)}, u32[]{:S(2)}) copy-start(f32[16,8192]{1,0:T(8,128)} %copy-done.40) | copy-start | bytes 1572868
  409.9 8.3 %collective-permute-start.23 = (f32[16,384]{1,0:T(8,128)S(1)}, f32[16,384]{1,0:T(8,128)S(1)}, u32[]{:S(2)}, u32[]{:S(2)}) collective-permute-start(f32[16,384]{1,0:T(8,128)S(1)} %get-tuple-element.22), channel_id=1, source_target_pairs={{0,8},{8,16},{16,24},{24,32},{32,40},{40,48},{48,56},{56,64},{64,7... | collective-permute-start | bytes 73736 | tf_op jit(solution)/shard_map/ppermute | solution.py:26
  413.6 6.0 %collective-permute-start.24 = (f32[16,384]{1,0:T(8,128)S(1)}, f32[16,384]{1,0:T(8,128)S(1)}, u32[]{:S(2)}, u32[]{:S(2)}) collective-permute-start(f32[16,384]{1,0:T(8,128)S(1)} %get-tuple-element.23), channel_id=1, source_target_pairs={{8,0},{16,8},{24,16},{32,24},{40,32},{48,40},{56,48},{64,56},{72,6... | collective-permute-start | bytes 73736 | tf_op jit(solution)/shard_map/ppermute | solution.py:27
  445.7 8.7 %collective-permute-start.25 = (f32[16,384]{1,0:T(8,128)S(1)}, f32[16,384]{1,0:T(8,128)S(1)}, u32[]{:S(2)}, u32[]{:S(2)}) collective-permute-start(f32[16,384]{1,0:T(8,128)S(1)} %get-tuple-element.20), channel_id=1, source_target_pairs={{0,8},{8,16},{16,24},{24,32},{32,40},{40,48},{48,56},{56,64},{64,7... | collective-permute-start | bytes 73736 | tf_op jit(solution)/shard_map/ppermute | solution.py:26
  449.4 6.0 %collective-permute-start.26 = (f32[16,384]{1,0:T(8,128)S(1)}, f32[16,384]{1,0:T(8,128)S(1)}, u32[]{:S(2)}, u32[]{:S(2)}) collective-permute-start(f32[16,384]{1,0:T(8,128)S(1)} %get-tuple-element.21), channel_id=1, source_target_pairs={{8,0},{16,8},{24,16},{32,24},{40,32},{48,40},{56,48},{64,56},{72,6... | collective-permute-start | bytes 73736 | tf_op jit(solution)/shard_map/ppermute | solution.py:27
  457.4 31.5 %copy-start.44 = (s32[1,8]{1,0:T(1,128)S(1)}, s32[1,8]{1,0:T(1,128)}, u32[]{:S(2)}) copy-start(s32[1,8]{1,0:T(1,128)} %param.9) | copy-start | bytes 100
  457.4 31.5 %copy-start.46 = (s32[8,1]{0,1:T(1,128)S(1)}, s32[8,1]{0,1:T(1,128)}, u32[]{:S(2)}) copy-start(s32[8,1]{0,1:T(1,128)} %copy-done.45) | copy-start | bytes 100
  480.6 9.0 %collective-permute-start.27 = (f32[16,384]{1,0:T(8,128)S(1)}, f32[16,384]{1,0:T(8,128)S(1)}, u32[]{:S(2)}, u32[]{:S(2)}) collective-permute-start(f32[16,384]{1,0:T(8,128)S(1)} %get-tuple-element.18), channel_id=1, source_target_pairs={{0,8},{8,16},{16,24},{24,32},{32,40},{40,48},{48,56},{56,64},{64,7... | collective-permute-start | bytes 73736 | tf_op jit(solution)/shard_map/ppermute | solution.py:26
  484.4 6.0 %collective-permute-start.28 = (f32[16,384]{1,0:T(8,128)S(1)}, f32[16,384]{1,0:T(8,128)S(1)}, u32[]{:S(2)}, u32[]{:S(2)}) collective-permute-start(f32[16,384]{1,0:T(8,128)S(1)} %get-tuple-element.19), channel_id=1, source_target_pairs={{8,0},{16,8},{24,16},{32,24},{40,32},{48,40},{56,48},{64,56},{72,6... | collective-permute-start | bytes 73736 | tf_op jit(solution)/shard_map/ppermute | solution.py:27
  516.4 10.9 %collective-permute-start.29 = (f32[16,384]{1,0:T(8,128)S(1)}, f32[16,384]{1,0:T(8,128)S(1)}, u32[]{:S(2)}, u32[]{:S(2)}) collective-permute-start(f32[16,384]{1,0:T(8,128)S(1)} %get-tuple-element.16), channel_id=1, source_target_pairs={{0,8},{8,16},{16,24},{24,32},{32,40},{40,48},{48,56},{56,64},{64,7... | collective-permute-start | bytes 73736 | tf_op jit(solution)/shard_map/ppermute | solution.py:26
  520.1 7.2 %collective-permute-start.30 = (f32[16,384]{1,0:T(8,128)S(1)}, f32[16,384]{1,0:T(8,128)S(1)}, u32[]{:S(2)}, u32[]{:S(2)}) collective-permute-start(f32[16,384]{1,0:T(8,128)S(1)} %get-tuple-element.17), channel_id=1, source_target_pairs={{8,0},{16,8},{24,16},{32,24},{40,32},{48,40},{56,48},{64,56},{72,6... | collective-permute-start | bytes 73736 | tf_op jit(solution)/shard_map/ppermute | solution.py:27
  529.3 23.3 %copy-start.16 = (f32[16,8192]{1,0:T(8,128)S(1)}, f32[16,8192]{1,0:T(8,128)}, u32[]{:S(2)}) copy-start(f32[16,8192]{1,0:T(8,128)} %copy-done.14) | copy-start | bytes 1572868
  529.3 23.3 %copy-start.25 = (f32[16,8192]{1,0:T(8,128)S(1)}, f32[16,8192]{1,0:T(8,128)}, u32[]{:S(2)}) copy-start(f32[16,8192]{1,0:T(8,128)} %get-tuple-element.11) | copy-start | bytes 1572868
  529.3 23.3 %copy-start.33 = (f32[64,2,8,128]{3,2,1,0:T(8,128)S(1)}, f32[64,2,8,128]{3,2,1,0:T(8,128)}, u32[]{:S(2)}) copy-start(f32[64,2,8,128]{3,2,1,0:T(8,128)} %copy-done.32) | copy-start | bytes 1572868
  529.3 23.3 %copy-start.39 = (f32[16,8192]{1,0:T(8,128)S(1)}, f32[16,8192]{1,0:T(8,128)}, u32[]{:S(2)}) copy-start(f32[16,8192]{1,0:T(8,128)} %copy-done.38) | copy-start | bytes 1572868
  (30 other events, 497.9 us)
